TPU v7x, 32 devices: a whole 2x2x4 slice. The times are simulated.
32 devices in a mesh: group: 4 (over z), dom: 8 (over y, x, core).
Axes of the slice: x: 2, y: 2, z: 4, core: 2. Of those that a mesh axis runs over, the one named last changes fastest.
Arguments:
- hot_rows: bfloat16 [4096, 1024], P(('group', 'dom')), may hold values from -6 to 6
- cold_codes: bfloat16 [4096, 1024], P(('group', 'dom')), may hold values from -127 to 127
- scale_index: int32 [4096], P(('group', 'dom')), may hold values from 0 to 255
- scale_table: float32 [256], replicated, may hold values from 0.004 to 0.04
- stale_rows: bfloat16 [4096, 1024], P(('group', 'dom')), may hold values from -6 to 6
- tile_index: int32 [64, 3], P(('group', 'dom')), may hold values from 0 to 2
- tile_count: int32 [64], P(('group', 'dom')), may hold values from 1 to 3
- tile_values: bfloat16 [64, 3, 128, 128], P(('group', 'dom')), may hold values from -0.3125 to 0.3125
- weight: bfloat16 [1024, 1024], P('dom'), may hold values from -0.1875 to 0.1875
- out_grad: bfloat16 [8192, 1024], P(('group', 'dom')), may hold values from -6 to 6
- stale_grads: bfloat16 [4096, 1024], P(('group', 'dom')), may hold values from -6 to 6
- send_rows: int32 [256, 16], P(('group', 'dom')), may hold values from 0 to 255
Outputs:
- activations: bfloat16 [8192, 1024], P(('group', 'dom'))
- feature_grad: bfloat16 [8192, 1024], P(('group', 'dom'))
- weight_grad: float32 [1024, 1024], P('dom')
- next_rows: bfloat16 [4096, 1024], P(('group', 'dom'))
- next_grads: bfloat16 [4096, 1024], P(('group', 'dom'))
Inputs may be any that keep to these rules, and one draw needn't show every extreme that they name: `send_rows`: rows may repeat.
All inputs are finite; a program needn't handle non-finite values.
Results may differ from a plain program's by a relative error of at most 0.0061.
Values may be sent and summed in bfloat16 or wider, within the bound.
A program may use at most 64 MiB of HBM per device.

v0:
```python
import jax
import jax.numpy as jnp
from jax import lax
from jax.sharding import PartitionSpec as P


def dequantize(cold_codes, scale_index, scale_table):
    levels = jnp.arange(scale_table.shape[0], dtype=jnp.int32)
    lookup = jnp.sum(
        jnp.where(
            scale_index[:, None] == levels[None, :],
            scale_table[None, :],
            jnp.zeros_like(scale_table)[None, :],
        ),
        axis=1,
    )
    return (cold_codes.astype(jnp.float32) * lookup[:, None]).astype(jnp.bfloat16)


def silu_parts(preact):
    logistic = jax.nn.sigmoid(preact)
    return (preact * logistic, logistic * (1.0 + preact * (1.0 - logistic)))


def local(
    hot_rows,
    cold_codes,
    scale_index,
    scale_table,
    stale_rows,
    tile_index,
    tile_count,
    tile_values,
    weight,
    out_grad,
    stale_grads,
    send_rows,
):
    tile_slots = tile_values.shape[1]
    cluster_rows = tile_values.shape[2]
    local_rows = jnp.concatenate(
        [hot_rows, dequantize(cold_codes, scale_index, scale_table)], axis=0
    )
    row_count = local_rows.shape[0]
    sends = send_rows.reshape(-1)
    outgoing = jnp.take(local_rows, sends, axis=0)
    next_rows = lax.all_to_all(outgoing, "dom", split_axis=0, concat_axis=0, tiled=True)
    source = jnp.concatenate([local_rows, stale_rows], axis=0)
    src_count = source.shape[0] // cluster_rows
    live_mask = jnp.arange(tile_slots, dtype=jnp.int32)[None, :] < tile_count[:, None]
    masked = jnp.where(
        live_mask[:, :, None, None], tile_values, jnp.zeros_like(tile_values)
    ).astype(jnp.float32)
    selector = (
        tile_index[:, :, None] == jnp.arange(src_count, dtype=jnp.int32)[None, None, :]
    ).astype(jnp.float32)
    operator = jnp.einsum("ckj,ckab->cajb", selector, masked, precision=lax.Precision.HIGHEST)
    operator = operator.reshape(row_count, src_count * cluster_rows)
    hidden = jnp.dot(operator, source.astype(jnp.float32), precision=lax.Precision.HIGHEST)
    hidden = hidden.astype(jnp.bfloat16)
    preact = jnp.dot(
        hidden,
        lax.all_gather(weight, "dom", axis=0, tiled=True),
        preferred_element_type=jnp.float32,
    )
    activ, slope = silu_parts(preact)
    activations = activ.astype(jnp.bfloat16)
    pre_grad = (out_grad.astype(jnp.float32) * slope).astype(jnp.bfloat16)
    hid_grad = lax.dot_general(
        pre_grad,
        lax.all_gather(weight, "dom", axis=0, tiled=True),
        (((1,), (1,)), ((), ())),
        preferred_element_type=jnp.float32,
    )
    hid_grad = hid_grad.astype(jnp.bfloat16)
    partial_value = lax.dot_general(
        hidden, pre_grad, (((0,), (0,)), ((), ())), preferred_element_type=jnp.float32
    )
    block_sum = lax.psum_scatter(partial_value, "dom", scatter_dimension=0, tiled=True)
    weight_grad = lax.psum(block_sum, "group")
    src_grad = lax.dot_general(
        operator,
        hid_grad.astype(jnp.float32),
        (((0,), (0,)), ((), ())),
        precision=lax.Precision.HIGHEST,
    )
    bound_grad = src_grad[row_count:].astype(jnp.bfloat16)
    next_grads = lax.all_to_all(bound_grad, "dom", split_axis=0, concat_axis=0, tiled=True)
    placing = (jnp.arange(row_count, dtype=jnp.int32)[:, None] == sends[None, :]).astype(
        jnp.bfloat16
    )
    returned = jnp.dot(placing, stale_grads, preferred_element_type=jnp.float32)
    feature_grad = (src_grad[:row_count] + returned).astype(jnp.bfloat16)
    return (activations, feature_grad, weight_grad, next_rows, next_grads)


def solution(mesh):
    placed = (
        P(("group", "dom"), None),
        P(("group", "dom"), None),
        P(("group", "dom")),
        P(),
        P(("group", "dom"), None),
        P(("group", "dom"), None),
        P(("group", "dom")),
        P(("group", "dom"), None, None, None),
        P("dom", None),
        P(("group", "dom"), None),
        P(("group", "dom"), None),
        P(("group", "dom"), None),
    )
    return jax.shard_map(
        local,
        mesh=mesh,
        in_specs=placed,
        out_specs=(
            P(("group", "dom"), None),
            P(("group", "dom"), None),
            P("dom", None),
            P(("group", "dom"), None),
            P(("group", "dom"), None),
        ),
        check_vma=False,
    )
```

profile of v0, /device:TPU:0, one launch (start us, length us, event | category | flops | bytes accessed | tf_op | source)
XLA Modules:
  0.0 148.6 jit_solution(3321438472732656839)
XLA Ops:
  7.2 0.0 copy-start
  7.2 0.0 all-gather.2.cloned.1.call-start
  7.2 0.7 all-gather.2.cloned.1.call-update
  7.9 0.0 reduce-scatter.2.cloned.1.call-start
  8.0 0.9 select_reduce_fusion
  8.8 0.7 iota_compare_fusion.4
  9.6 1.0 broadcast_select_fusion.1
  10.6 1.1 multiply_convert_fusion.2
  11.6 1.0 fusion.11
  12.6 2.0 %convolution_convert_fusion = bf16[256,1024]{1,0:T(8,128)(2,1)S(1)} fusion(bf16[128,1024]{1,0:T(8,128)(2,1)} %param.16, bf16[128,1024]{1,0:T(8,128)(2,1)S(1)} %multiply_convert_fusion.2, bf16[128,1024]{1,0:T(8,128)(2,1)} %param.12, f32[32,8,3,128]{3,2,1,0:T(4,128)S(1)} %bitcast.25), kind=kOutput, calls=%fused_computation.2 | convolution fusion | flops 1210580992 | bytes 1703936 | tf_op jit(solution)/shard_map/dot_general | solution.py:59
  14.6 0.0 copy-start.1
  14.6 25.8 %all-gather.2.cloned.1.call-done = bf16[1024,1024]{1,0:T(8,128)(2,1)} async-done(((bf16[128,1024]{1,0:T(8,128)(2,1)}), bf16[1024,1024]{1,0:T(8,128)(2,1)}) %all-gather.2.cloned.1.call-update) | async-done | bytes 2097168 | tf_op jit(solution)/shard_map/all_gather | solution.py:63
  40.4 3.2 %multiply_convert_fusion.1 = (bf16[256,1024]{1,0:T(8,128)(2,1)}, f32[256,1024]{1,0:T(8,128)S(1)}) fusion(bf16[256,1024]{1,0:T(8,128)(2,1)S(1)} %convolution_convert_fusion, bf16[1024,1024]{1,0:T(8,128)(2,1)} %all-gather.2.cloned.1.call-done), kind=kOutput, calls=%fused_computation.6 | convolution fusion | flops 538181632 | bytes 4194304 | tf_op jit(solution)/shard_map/dot_general | solution.py:61
  43.6 0.0 copy-done.1
  43.6 2.9 %fusion.19 = f32[1024,1024]{1,0:T(8,128)} fusion(bf16[256,1024]{1,0:T(8,128)(2,1)S(1)} %convolution_convert_fusion, f32[256,1024]{1,0:T(8,128)S(1)} %get-tuple-element.6, bf16[256,1024]{1,0:T(8,128)(2,1)S(1)} %copy-done.1), kind=kOutput, calls=%fused_computation.39 | convolution fusion | flops 539492352 | bytes 6291456 | tf_op jit(solution)/shard_map/dot_general | solution.py:76
  46.5 0.0 copy-start.3
  46.5 0.0 copy-start.2
  46.5 0.0 reduce-scatter.2.cloned.1.call-update
  46.5 0.7 copy-done.3
  47.1 0.1 reshape.86
  47.2 0.2 copy-done.2
  47.5 0.9 gather_fusion
  48.3 0.8 broadcast_select_fusion
  49.1 3.4 %all-to-all-start = ((bf16[8,16,1024]{2,1,0:T(8,128)(2,1)}), bf16[8,16,1024]{2,1,0:T(8,128)(2,1)S(1)}, u32[]{:S(2)}, u32[]{:S(2)}) async-start(bf16[8,16,1024]{2,1,0:T(8,128)(2,1)} %broadcast_select_fusion), calls=%async_computation.1 | async-start | bytes 524288 | tf_op jit(solution)/shard_map/all_to_all | solution.py:47
  52.5 0.0 all-reduce.2.cloned.1.call-start
  52.6 0.1 eq.48
  52.7 6.7 %all-to-all-done = bf16[8,16,1024]{2,1,0:T(8,128)(2,1)S(1)} async-done(((bf16[8,16,1024]{2,1,0:T(8,128)(2,1)}), bf16[8,16,1024]{2,1,0:T(8,128)(2,1)S(1)}, u32[]{:S(2)}, u32[]{:S(2)}) %all-to-all-start) | async-done | bytes 262176 | tf_op jit(solution)/shard_map/all_to_all | solution.py:47
  59.4 3.3 %convolution_convert_fusion.1 = bf16[256,1024]{1,0:T(8,128)(2,1)} fusion(bf16[1024,1024]{1,0:T(8,128)(2,1)} %all-gather.2.cloned.1.call-done, f32[256,1024]{1,0:T(8,128)S(1)} %get-tuple-element.6, bf16[256,1024]{1,0:T(8,128)(2,1)S(1)} %copy-done.1), kind=kOutput, calls=%fused_computation.4 | convolution fusion | flops 539754496 | bytes 4194304 | tf_op jit(solution)/shard_map/dot_general | solution.py:69
  62.7 35.0 %reduce-scatter.2.cloned.1.call-done = f32[128,1024]{1,0:T(8,128)} async-done(((f32[1024,1024]{1,0:T(8,128)}), f32[128,1024]{1,0:T(8,128)}) %reduce-scatter.2.cloned.1.call-update) | async-done | bytes 524304 | tf_op jit(solution)/shard_map/reduce_scatter | solution.py:79
  97.8 0.0 all-reduce.2.cloned.1.call-update
  97.8 1.9 %fusion.7 = f32[384,1024]{1,0:T(8,128)S(1)} fusion(bf16[256,1024]{1,0:T(8,128)(2,1)} %convolution_convert_fusion.1, f32[32,8,3,128]{3,2,1,0:T(4,128)S(1)} %bitcast.26), kind=kOutput, calls=%fused_computation.17 | convolution fusion | flops 1207959552 | bytes 2490368 | tf_op jit(solution)/shard_map/dot_general | solution.py:81
  99.7 0.7 slice.15
  100.4 3.4 %all-to-all-start.1 = ((bf16[8,16,1024]{2,1,0:T(8,128)(2,1)}), bf16[8,16,1024]{2,1,0:T(8,128)(2,1)S(1)}, u32[]{:S(2)}, u32[]{:S(2)}) async-start(bf16[8,16,1024]{2,1,0:T(8,128)(2,1)} %bitcast.6), calls=%async_computation.2 | async-start | bytes 524288 | tf_op jit(solution)/shard_map/all_to_all | solution.py:88
  103.8 0.0 copy-done
  103.8 1.1 fusion
  104.9 5.7 %all-to-all-done.1 = bf16[8,16,1024]{2,1,0:T(8,128)(2,1)S(1)} async-done(((bf16[8,16,1024]{2,1,0:T(8,128)(2,1)}), bf16[8,16,1024]{2,1,0:T(8,128)(2,1)S(1)}, u32[]{:S(2)}, u32[]{:S(2)}) %all-to-all-start.1) | async-done | bytes 262176 | tf_op jit(solution)/shard_map/all_to_all | solution.py:88
  110.7 28.1 %all-reduce.2.cloned.1.call-done = f32[128,1024]{1,0:T(8,128)} async-done(((f32[128,1024]{1,0:T(8,128)}), f32[128,1024]{1,0:T(8,128)}) %all-reduce.2.cloned.1.call-update) | async-done | bytes 524304 | tf_op jit(solution)/shard_map/psum | solution.py:80
  138.8 1.9 %copy.38 = f32[128,1024]{1,0:T(8,128)} copy(f32[128,1024]{1,0:T(8,128)} %all-reduce.2.cloned.1.call-done) | data formatting | bytes 1048576
  140.7 0.7 copy.39
  141.4 0.7 copy.40
  (4 shorter events, 0.1 us)
Async XLA Ops:
  7.2 96.7 %copy-start = (bf16[128,1024]{1,0:T(8,128)(2,1)S(1)}, bf16[128,1024]{1,0:T(8,128)(2,1)}, u32[]{:S(2)}) copy-start(bf16[128,1024]{1,0:T(8,128)(2,1)} %param.22) | copy-start | bytes 786436
  7.2 33.2 %all-gather.2.cloned.1.call-start = ((), (), s32[]{:S(2)}) async-start(), calls=%async_computation.3 | async-start | bytes 2359296 | tf_op jit(solution)/shard_map/all_gather | solution.py:63
  7.9 89.9 %reduce-scatter.2.cloned.1.call-start = ((), (), s32[]{:S(2)}) async-start(), calls=%async_computation.4 | async-start | bytes 4718592 | tf_op jit(solution)/shard_map/reduce_scatter | solution.py:79
  14.6 29.0 %copy-start.1 = (bf16[256,1024]{1,0:T(8,128)(2,1)S(1)}, bf16[256,1024]{1,0:T(8,128)(2,1)}, u32[]{:S(2)}) copy-start(bf16[256,1024]{1,0:T(8,128)(2,1)} %param.21) | copy-start | bytes 1572868
  46.5 0.7 copy-start.3
  46.5 1.0 copy-start.2
  49.1 10.3 %all-to-all-start = ((bf16[8,16,1024]{2,1,0:T(8,128)(2,1)}), bf16[8,16,1024]{2,1,0:T(8,128)(2,1)S(1)}, u32[]{:S(2)}, u32[]{:S(2)}) async-start(bf16[8,16,1024]{2,1,0:T(8,128)(2,1)} %broadcast_select_fusion), calls=%async_computation.1 | async-start | bytes 524288 | tf_op jit(solution)/shard_map/all_to_all | solution.py:47
  52.5 86.3 %all-reduce.2.cloned.1.call-start = ((), (), s32[]{:S(2)}) async-start(), calls=%async_computation.5 | async-start | bytes 1048576 | tf_op jit(solution)/shard_map/psum | solution.py:80
  100.4 10.3 %all-to-all-start.1 = ((bf16[8,16,1024]{2,1,0:T(8,128)(2,1)}), bf16[8,16,1024]{2,1,0:T(8,128)(2,1)S(1)}, u32[]{:S(2)}, u32[]{:S(2)}) async-start(bf16[8,16,1024]{2,1,0:T(8,128)(2,1)} %bitcast.6), calls=%async_computation.2 | async-start | bytes 524288 | tf_op jit(solution)/shard_map/all_to_all | solution.py:88
Sparse Core Ops, SparseCore 0:
  9.9 30.4 all-gather.1
  46.6 51.1 reduce-scatter.1
  100.1 38.6 all-reduce.1
where the time goes:
time: 149 us
  waiting for transfers between devices  102 us (68%)
  matrix products  15.3 us (10%)
  between operations  13.8 us (9%)
  starting transfers between devices  6.95 us (5%)
  local copies, waits for them, and re-layouts  5.91 us (4%)
  other arithmetic  4.51 us (3%)
    reduce_scatter x1, waiting for transfers between devices, local(): lax.psum_scatter(partial_value, 'dom', scatter_dimension=0, tiled=True)  35 us
    psum x1, waiting for transfers between devices, local(): weight_grad = lax.psum(block_sum, 'group')  28.1 us
    all_gather x1, waiting for transfers between devices, local(): lax.all_gather(weight, 'dom', axis=0, tiled=True)  25.8 us
    all_to_all x1, waiting for transfers between devices, local(): lax.all_to_all(outgoing, 'dom', split_axis=0, concat_axis=0, tiled=True)  6.71 us
    all_to_all x1, waiting for transfers between devices, local(): lax.all_to_all(bound_grad, 'dom', split_axis=0, concat_axis=0, tiled=True)  5.75 us
    unnamed x11, local copies, waits for them, and re-layouts  4.15 us
    all_to_all x1, starting transfers between devices, local(): lax.all_to_all(outgoing, 'dom', split_axis=0, concat_axis=0, tiled=True)  3.42 us
    all_to_all x1, starting transfers between devices, local(): lax.all_to_all(bound_grad, 'dom', split_axis=0, concat_axis=0, tiled=True)  3.41 us
  transfers between devices with their start and end apart: 5, of which 5 were waited for; matrix products, arithmetic and copies ran while one was open for 10% of the time, Pallas kernels for 0%

commit v1 on v0

v1 whole, which is shorter than its diff:
```python
import functools

import jax
import jax.numpy as jnp
from jax import lax
from jax.experimental import pallas as pl
from jax.experimental.pallas import tpu as pltpu
from jax.sharding import PartitionSpec as P

MESH = pl.DeviceIdType.MESH
F32, BF16 = jnp.float32, jnp.bfloat16
NT = (((1,), (1,)), ((), ()))


def each(lo, hi, body):
    if hi - lo <= 8:
        for i in range(lo, hi):
            body(i)
    else:
        pl.loop(lo, hi)(body)


def pieces(n_group, blk, depth):
    nc = min(n_group, depth // 128)
    sub = n_group // nc
    return nc, sub, blk // sub, depth // nc


def mm(a, b):
    return jnp.dot(a, b, preferred_element_type=F32)


def kernel(
    n_group, n_dom,
    tidx_ref, tcnt_ref, hot_ref, cold_ref, sidx_ref, table_ref, stale_ref, tile_ref, w_ref,
    og_ref, sg_ref, send_ref,
    act_ref, fg_ref, wg_ref, nr_ref, ng_ref,
    src, wbuf, hid, hid_t, pre, ptx, prx, own, stx, rrx, ztx, zrx, ftx, frx, acc, rowsf, outx, bgx,
    op_hi, op_lo, hgrad,
    ag_s, ag_r, pa_s, pa_r, nr_s, nr_r, ng_s, ng_r, pt_s, pt_r, st_s, st_r, z_s, z_r, f_s, f_r,
):
    g, d = lax.axis_index("group"), lax.axis_index("dom")
    n_pair = n_dom // 2
    pair, core = d // 2, d % 2
    partner = pair * 2 + (1 - core)
    blk, depth = w_ref.shape
    nc, sub, bs, cw = pieces(n_group, blk, depth)
    n_cl, slots, cl, _ = tile_ref.shape
    n_src = src.shape[0]
    rows = n_cl * cl
    peer = send_ref.shape[1]
    sends = n_dom * peer

    barrier = pltpu.get_barrier_semaphore()

    def hello_dom(r):
        pl.semaphore_signal(barrier, inc=1, device_id={"dom": (d + r) % n_dom}, device_id_type=MESH)

    def hello_group(r):
        pl.semaphore_signal(barrier, inc=1, device_id={"group": (g + r) % n_group}, device_id_type=MESH)

    each(1, n_dom, hello_dom)
    each(1, n_group, hello_group)
    pl.semaphore_wait(barrier, n_dom + n_group - 2)

    def remote(source, target, send_sem, recv_sem, where):
        return pltpu.make_async_remote_copy(
            src_ref=source, dst_ref=target, send_sem=send_sem, recv_sem=recv_sem,
            device_id=where, device_id_type=MESH)

    def chunk(i):
        return (g // sub + 1 + i) % nc

    def cols(ch):
        return pl.ds(pl.multiple_of(ch * cw, cw), cw)

    def ag_copy(ch, r):
        q = (pair + r) % n_pair
        return remote(w_ref.at[:, cols(ch)], wbuf.at[ch, d], ag_s.at[ch, r], ag_r.at[ch, r],
                      {"dom": q * 2 + core})

    def pa_first(ch):
        return remote(w_ref.at[:, cols(ch)], wbuf.at[ch, d], pa_s.at[ch, 0], pa_r.at[ch, 0],
                      {"dom": partner})

    def pa_copy(ch, r):
        slot = ((pair - r + n_pair) % n_pair) * 2 + core
        return remote(wbuf.at[ch, slot], wbuf.at[ch, slot], pa_s.at[ch, r], pa_r.at[ch, r],
                      {"dom": partner})

    for i in range(nc):
        each(1, n_pair, lambda r: ag_copy(chunk(i), r).start())
        pa_first(chunk(i)).start()
    for i in range(nc):
        wbuf[i, d] = w_ref[:, i * cw:(i + 1) * cw]

    spread = jnp.broadcast_to(sidx_ref[...].astype(F32), (cl, cl)).T
    scale = jnp.zeros((cl, 1), F32)
    for h in range(table_ref.shape[1] // cl):
        level = (lax.broadcasted_iota(jnp.int32, (cl, cl), 1) + h * cl).astype(F32)
        entry = jnp.broadcast_to(table_ref[:, h * cl:(h + 1) * cl], (cl, cl))
        scale = scale + jnp.sum(jnp.where(spread == level, entry, 0.0), axis=1, keepdims=True)
    src[0] = hot_ref[...]
    src[1] = (cold_ref[...].astype(F32) * scale).astype(BF16)
    src[2] = stale_ref[...]

    lift = (lax.broadcasted_iota(jnp.int32, (sends, n_dom), 0) // peer
            == lax.broadcasted_iota(jnp.int32, (sends, n_dom), 1)).astype(F32)
    wide = jnp.dot(lift, send_ref[...].astype(F32), precision=lax.Precision.HIGHEST,
                   preferred_element_type=F32)
    place = (lax.broadcasted_iota(jnp.int32, (sends, peer), 0) % peer
             == lax.broadcasted_iota(jnp.int32, (sends, peer), 1))
    listed = jnp.sum(jnp.where(place, wide, 0.0), axis=1, keepdims=True)
    picks = (listed == lax.broadcasted_iota(jnp.int32, (sends, rows), 1).astype(F32)).astype(F32)
    own_rows = jnp.concatenate([src[0], src[1]], axis=0)
    rowsf[...] = mm(picks.astype(BF16), own_rows)
    for p in range(n_dom):
        outx[p] = rowsf[p * peer:(p + 1) * peer, :].astype(BF16)
    nr_ref[d] = outx[d]

    def nr_copy(r):
        p = (d + r) % n_dom
        return remote(outx.at[p], nr_ref.at[d], nr_s.at[r], nr_r.at[r], {"dom": p})

    for c in range(n_cl):
        total = jnp.zeros((cl, depth), F32)
        for k in range(slots):
            tile = jnp.where(jnp.full((cl, cl), tcnt_ref[c], jnp.int32) > k, tile_ref[c, k], 0)
            total = total + mm(tile, src[tidx_ref[c, k]])
        hid[c * cl:(c + 1) * cl, :] = total.astype(BF16)
    turned = hid[...].astype(F32).T.astype(BF16)
    hid_t[...] = turned.reshape(n_pair, 2, blk, rows)
    for c in range(n_cl):
        for j in range(n_src):
            part = jnp.zeros((cl, cl), F32)
            for k in range(slots):
                live = (jnp.full((cl, cl), tcnt_ref[c], jnp.int32) > k) & (
                    jnp.full((cl, cl), tidx_ref[c, k], jnp.int32) == j)
                part = part + jnp.where(live, tile_ref[c, k].astype(F32), 0.0)
            part = part.T
            high = part.astype(BF16)
            op_hi[j, :, c * cl:(c + 1) * cl] = high
            op_lo[j, :, c * cl:(c + 1) * cl] = (part - high.astype(F32)).astype(BF16)

    def pt_copy(ch):
        return remote(ptx.at[ch], prx.at[ch], pt_s.at[ch], pt_r.at[ch], {"dom": partner})

    def st_copy(ch, r):
        q = (pair + r) % n_pair
        return remote(stx.at[ch, q], rrx.at[ch, r], st_s.at[ch, r], st_r.at[ch, r],
                      {"dom": q * 2 + core})

    def z_copy(r):
        to = (g + r) % n_group
        return remote(ztx.at[to // sub, to % sub], zrx.at[r], z_s.at[r], z_r.at[r], {"group": to})

    def f_copy(r):
        return remote(ftx, frx.at[r], f_s.at[r], f_r.at[r], {"group": (g + r) % n_group})

    def stage_a(i):
        ch = chunk(i)

        def relay(r):
            ag_copy(ch, r).wait_recv()
            pa_copy(ch, r).start()

        each(1, n_pair, relay)
        pa_first(ch).wait_recv()
        each(1, n_pair, lambda r: pa_copy(ch, r).wait_recv())
        weight = wbuf[ch].reshape(depth, cw)
        preact = mm(hid[...], weight)
        s = jax.nn.sigmoid(preact)
        act_ref[:, cols(ch)] = (preact * s).astype(BF16)
        slope = s * (1.0 + preact * (1.0 - s))
        pg = (og_ref[:, cols(ch)].astype(F32) * slope).astype(BF16)
        pre[ch] = pg
        away = mm(hid_t[:, 1 - core].reshape(n_pair * blk, rows), pg)
        ptx[ch] = away.astype(BF16).reshape(n_pair, blk, cw)
        pt_copy(ch).start()
        here = mm(hid_t[:, core].reshape(n_pair * blk, rows), pg)
        own[ch] = here.reshape(n_pair, blk, cw)

    def stage_b(i):
        ch = chunk(i)
        pt_copy(ch).wait_recv()
        stx[ch] = (own[ch] + prx[ch].astype(F32)).astype(BF16)
        each(1, n_pair, lambda r: st_copy(ch, r).start())
        acc[i] = (own[ch, pair] + prx[ch, pair].astype(F32)).reshape(sub, bs, cw)

    def stage_c(i):
        ch = chunk(i)

        def add(r):
            st_copy(ch, r).wait_recv()
            acc[i] = acc[i] + rrx[ch, r].astype(F32).reshape(sub, bs, cw)

        each(1, n_pair, add)
        ztx[ch] = acc[i].astype(BF16)
        for h in range(sub):
            if i < nc - 1:
                z_copy((ch * sub + h - g + n_group) % n_group).start()
            elif h > 0:
                mate = ch * sub + (g + h) % sub
                z_copy((mate - g + n_group) % n_group).start()

    for i in range(nc):
        stage_a(i)
        if i >= 1:
            stage_b(i - 1)
        if i == 0:
            each(1, n_dom, lambda r: nr_copy(r).start())
        if i >= 2:
            stage_c(i - 2)

    def back(m):
        part = jnp.zeros((rows, cw), F32)
        for c in range(nc):
            wpart = wbuf[c].reshape(depth, cw)[m * cw:(m + 1) * cw]
            part = part + lax.dot_general(pre[c], wpart, NT, preferred_element_type=F32)
        hgrad[:, m * cw:(m + 1) * cw] = part.astype(BF16)

    for m in range(nc):
        back(m)
        if m == 0:
            stage_b(nc - 1)

    def source_grad(j):
        return mm(op_hi[j], hgrad[...]) + mm(op_lo[j], hgrad[...])

    rowsf[...] = source_grad(n_src - 1)
    for p in range(n_dom):
        bgx[p] = rowsf[p * peer:(p + 1) * peer, :].astype(BF16)
    ng_ref[d] = bgx[d]

    def ng_copy(r):
        p = (d + r) % n_dom
        return remote(bgx.at[p], ng_ref.at[d], ng_s.at[r], ng_r.at[r], {"dom": p})

    each(1, n_dom, lambda r: ng_copy(r).start())
    if nc >= 2:
        stage_c(nc - 2)
    stage_c(nc - 1)

    def gather(r):
        z_copy(r).wait_recv()
        acc[nc - 1, g % sub] = acc[nc - 1, g % sub] + zrx[r].astype(F32)

    each(1, n_group, gather)
    ftx[...] = acc[nc - 1, g % sub].astype(BF16)
    each(1, n_group, lambda r: f_copy(r).start())

    def store(owner, value):
        wg_ref[pl.ds(pl.multiple_of(owner % sub * bs, bs), bs), cols(owner // sub)] = value.astype(F32)

    store(g, ftx[...])

    for j in range(n_src - 1):
        back_rows = lax.dot_general(
            picks[:, j * cl:(j + 1) * cl].T.astype(BF16), sg_ref[...], (((1,), (0,)), ((), ())),
            preferred_element_type=F32)
        fg_ref[j * cl:(j + 1) * cl, :] = (source_grad(j) + back_rows).astype(BF16)

    def take(r):
        f_copy(r).wait_recv()
        store((g - r + n_group) % n_group, frx[r])

    each(1, n_group, take)

    def drain_dom(r):
        nr_copy(r).wait()
        ng_copy(r).wait()

    each(1, n_dom, drain_dom)
    for i in range(nc):
        ch = chunk(i)

        def drain(r):
            ag_copy(ch, r).wait_send()
            pa_copy(ch, r).wait_send()
            st_copy(ch, r).wait_send()

        each(1, n_pair, drain)
        pa_first(ch).wait_send()
        pt_copy(ch).wait_send()

    def drain_group(r):
        z_copy(r).wait_send()
        f_copy(r).wait_send()

    each(1, n_group, drain_group)


def local(n_group, n_dom, hot_rows, cold_codes, scale_index, scale_table, stale_rows, tile_index,
          tile_count, tile_values, weight, out_grad, stale_grads, send_rows):
    blk, depth = weight.shape
    rows = out_grad.shape[0]
    cl = tile_values.shape[2]
    peer = send_rows.shape[1]
    n_pair = n_dom // 2
    nc, sub, bs, cw = pieces(n_group, blk, depth)
    n_src = rows // cl + stale_rows.shape[0] // cl
    vmem, smem = pl.BlockSpec(memory_space=pltpu.VMEM), pl.BlockSpec(memory_space=pltpu.SMEM)
    dma = pltpu.SemaphoreType.DMA
    out = pl.pallas_call(
        functools.partial(kernel, n_group, n_dom),
        out_shape=(
            jax.ShapeDtypeStruct((rows, depth), BF16),
            jax.ShapeDtypeStruct((rows, depth), BF16),
            jax.ShapeDtypeStruct((blk, depth), F32),
            jax.ShapeDtypeStruct((n_dom, peer, depth), BF16),
            jax.ShapeDtypeStruct((n_dom, peer, depth), BF16),
        ),
        in_specs=[smem] * 2 + [vmem] * 10,
        out_specs=(vmem,) * 5,
        scratch_shapes=[
            pltpu.VMEM((n_src, cl, depth), BF16),
            pltpu.VMEM((nc, n_dom, blk, cw), BF16),
            pltpu.VMEM((rows, depth), BF16),
            pltpu.VMEM((n_pair, 2, blk, rows), BF16),
            pltpu.VMEM((nc, rows, cw), BF16),
            pltpu.VMEM((nc, n_pair, blk, cw), BF16),
            pltpu.VMEM((nc, n_pair, blk, cw), BF16),
            pltpu.VMEM((nc, n_pair, blk, cw), F32),
            pltpu.VMEM((nc, n_pair, blk, cw), BF16),
            pltpu.VMEM((nc, n_pair, blk, cw), BF16),
            pltpu.VMEM((nc, sub, bs, cw), BF16),
            pltpu.VMEM((n_group, bs, cw), BF16),
            pltpu.VMEM((bs, cw), BF16),
            pltpu.VMEM((n_group, bs, cw), BF16),
            pltpu.VMEM((nc, sub, bs, cw), F32),
            pltpu.VMEM((n_dom * peer, depth), F32),
            pltpu.VMEM((n_dom, peer, depth), BF16),
            pltpu.VMEM((n_dom, peer, depth), BF16),
            pltpu.VMEM((n_src, cl, rows), BF16),
            pltpu.VMEM((n_src, cl, rows), BF16),
            pltpu.VMEM((rows, depth), BF16),
            dma((nc, n_pair)), dma((nc, n_pair)), dma((nc, n_pair)), dma((nc, n_pair)),
            dma((n_dom,)), dma((n_dom,)), dma((n_dom,)), dma((n_dom,)),
            dma((nc,)), dma((nc,)), dma((nc, n_pair)), dma((nc, n_pair)),
            dma((n_group,)), dma((n_group,)), dma((n_group,)), dma((n_group,)),
        ],
        compiler_params=pltpu.CompilerParams(
            collective_id=0, has_side_effects=True, vmem_limit_bytes=48 * 1024 * 1024),
    )(tile_index, tile_count, hot_rows, cold_codes, scale_index.reshape(1, -1),
      scale_table.reshape(1, -1), stale_rows, tile_values, weight, out_grad, stale_grads, send_rows)
    act, fg, wg, nr, ng = out
    return act, fg, wg, nr.reshape(-1, depth), ng.reshape(-1, depth)


def solution(mesh):
    both = ("group", "dom")
    return jax.shard_map(
        functools.partial(local, mesh.shape["group"], mesh.shape["dom"]),
        mesh=mesh,
        in_specs=(
            P(both, None), P(both, None), P(both), P(), P(both, None), P(both, None), P(both),
            P(both, None, None, None), P("dom", None), P(both, None), P(both, None), P(both, None),
        ),
        out_specs=(P(both, None), P(both, None), P("dom", None), P(both, None), P(both, None)),
        check_vma=False,
    )
```

time: 149 us -> 57.4 us (0.39)
  waiting for transfers between devices: 102 us -> 0 us
  Pallas kernels: 0 us -> 44.5 us
  matrix products: 15.3 us -> 0 us
  between operations: 13.8 us -> 0.69 us
  starting transfers between devices: 6.95 us -> 0 us
  local copies, waits for them, and re-layouts: 5.91 us -> 11.9 us
  other arithmetic: 4.51 us -> 0 us
    pallas_call x0 -> x1, Pallas kernels: none -> 44.5 us  [local(): pl.pallas_call(functools.partial(kernel, n_group, n_dom), out_shape=(jax....]
    reduce_scatter x1 -> x0, waiting for transfers between devices: 35 us -> none  [local(): lax.psum_scatter(partial_value, 'dom', scatter_dimension=0, tiled=True)]
    psum x1 -> x0, waiting for transfers between devices: 28.1 us -> none  [local(): weight_grad = lax.psum(block_sum, 'group')]
    all_gather x1 -> x0, waiting for transfers between devices: 25.8 us -> none  [local(): lax.all_gather(weight, 'dom', axis=0, tiled=True)]
    dot_general x7 -> x0, matrix products: 15.3 us -> none  [the longest x1 3.34 us: local(): lax.dot_general(pre_grad, lax.all_gather(weight, 'dom', axis=0, tiled=Tru...]
    all_to_all x2 -> x0, waiting for transfers between devices: 12.5 us -> none  [the longest x1 6.71 us: local(): lax.all_to_all(outgoing, 'dom', split_axis=0, concat_axis=0, tiled=True)]
    unnamed x11 -> x29, local copies, waits for them, and re-layouts: 4.15 us -> 11.9 us
    all_to_all x2 -> x0, starting transfers between devices: 6.83 us -> none  [the longest x1 3.42 us: local(): lax.all_to_all(outgoing, 'dom', split_axis=0, concat_axis=0, tiled=True)]
  transfers between devices with their start and end apart: 5 -> 0, of which waited for: 5 -> 0; matrix products, arithmetic and copies ran while one was open for 10% -> 0% of each run, Pallas kernels for 0% -> 0%
where the time goes in v1:
time: 57.4 us; the launch traced here: 57 us
  Pallas kernels  44.5 us (78%)
  local copies, waits for them, and re-layouts  11.9 us (21%)
  between operations  0.69 us (1%)
    pallas_call x1, Pallas kernels, local(): pl.pallas_call(functools.partial(kernel, n_group, n_dom), out_shape=(jax....  44.5 us
    unnamed x29, local copies, waits for them, and re-layouts  11.9 us

profile of v1, /device:TPU:0, one launch (start us, length us, event | category | flops | bytes accessed | tf_op | source)
XLA Modules:
  0.0 57.0 jit_solution(7095931148059045210)
XLA Ops:
  0.6 0.0 copy-start.9
  0.6 0.0 copy-start.11
  0.7 0.0 copy-start.8
  0.7 0.0 copy-start.10
  0.7 0.6 %copy-done.9 = f32[256]{0:T(256)S(1)} copy-done((f32[256]{0:T(256)S(1)}, f32[256]{0:T(256)}, u32[]{:S(2)}) %copy-start.9) | copy-done | bytes 1048
  1.3 0.0 copy-done.11
  1.3 0.0 copy-done.8
  1.3 0.0 copy-done.10
  1.4 0.0 copy-start
  1.4 1.0 %copy-done = bf16[256,1024]{1,0:T(8,128)(2,1)S(1)} copy-done((bf16[256,1024]{1,0:T(8,128)(2,1)S(1)}, bf16[256,1024]{1,0:T(8,128)(2,1)}, u32[]{:S(2)}) %copy-start) | copy-done | bytes 524312
  2.4 0.0 copy-start.1
  2.4 0.9 %copy-done.1 = bf16[128,1024]{1,0:T(8,128)(2,1)S(1)} copy-done((bf16[128,1024]{1,0:T(8,128)(2,1)S(1)}, bf16[128,1024]{1,0:T(8,128)(2,1)}, u32[]{:S(2)}) %copy-start.1) | copy-done | bytes 262168
  3.3 0.0 copy-start.2
  3.3 0.9 %copy-done.2 = bf16[128,1024]{1,0:T(8,128)(2,1)S(1)} copy-done((bf16[128,1024]{1,0:T(8,128)(2,1)S(1)}, bf16[128,1024]{1,0:T(8,128)(2,1)}, u32[]{:S(2)}) %copy-start.2) | copy-done | bytes 262168
  4.3 0.0 copy-start.3
  4.3 0.9 %copy-done.3 = bf16[128,1024]{1,0:T(8,128)(2,1)S(1)} copy-done((bf16[128,1024]{1,0:T(8,128)(2,1)S(1)}, bf16[128,1024]{1,0:T(8,128)(2,1)}, u32[]{:S(2)}) %copy-start.3) | copy-done | bytes 262168
  5.2 0.0 copy-start.4
  5.2 0.9 %copy-done.4 = bf16[128,1024]{1,0:T(8,128)(2,1)S(1)} copy-done((bf16[128,1024]{1,0:T(8,128)(2,1)S(1)}, bf16[128,1024]{1,0:T(8,128)(2,1)}, u32[]{:S(2)}) %copy-start.4) | copy-done | bytes 262168
  6.2 0.0 copy-start.5
  6.2 0.9 %copy-done.5 = bf16[128,1024]{1,0:T(8,128)(2,1)S(1)} copy-done((bf16[128,1024]{1,0:T(8,128)(2,1)S(1)}, bf16[128,1024]{1,0:T(8,128)(2,1)}, u32[]{:S(2)}) %copy-start.5) | copy-done | bytes 262168
  7.1 0.0 copy-start.6
  7.1 0.9 %copy-done.6 = bf16[2,3,128,128]{3,2,1,0:T(8,128)(2,1)S(1)} copy-done((bf16[2,3,128,128]{3,2,1,0:T(8,128)(2,1)S(1)}, bf16[2,3,128,128]{3,2,1,0:T(8,128)(2,1)}, u32[]{:S(2)}) %copy-start.6) | copy-done | bytes 196632
  8.1 0.0 copy-start.7
  8.1 0.7 %copy-done.7 = s32[8,16]{1,0:T(8,128)S(1)} copy-done((s32[8,16]{1,0:T(8,128)S(1)}, s32[8,16]{1,0:T(8,128)}, u32[]{:S(2)}) %copy-start.7) | copy-done | bytes 536
  8.8 44.5 %shard_map.155 = (bf16[256,1024]{1,0:T(8,128)(2,1)S(1)}, bf16[256,1024]{1,0:T(8,128)(2,1)S(1)}, f32[128,1024]{1,0:T(8,128)S(1)}, bf16[8,16,1024]{2,1,0:T(8,128)(2,1)S(1)}, bf16[8,16,1024]{2,1,0:T(8,128)(2,1)S(1)}) custom-call(s32[2,3]{1,0:T(2,128)S(1)} %copy-done.8, s32[2]{0:T(128)S(1)} %copy-done.10, bf16[128,1024]{1,0:T(8,128)(2,1)S(1)} %copy-done.1, ...), custom_call_target="tpu_custom_call" | custom-call | tf_op jit(solution)/shard_map/pallas_call | solution.py:304
  53.2 0.8 %copy.22 = bf16[256,1024]{1,0:T(8,128)(2,1)} copy(bf16[256,1024]{1,0:T(8,128)(2,1)S(1)} %get-tuple-element.20) | data formatting | bytes 1048576
  54.0 0.8 %copy.23 = bf16[256,1024]{1,0:T(8,128)(2,1)} copy(bf16[256,1024]{1,0:T(8,128)(2,1)S(1)} %get-tuple-element.21) | data formatting | bytes 1048576
  54.8 0.8 %copy.24 = f32[128,1024]{1,0:T(8,128)} copy(f32[128,1024]{1,0:T(8,128)S(1)} %get-tuple-element.22) | data formatting | bytes 1048576
  55.6 0.7 %copy.25 = bf16[128,1024]{1,0:T(8,128)(2,1)} copy(bf16[128,1024]{1,0:T(8,128)(2,1)S(1)} %bitcast.5) | data formatting | bytes 524288
  56.3 0.7 %copy.26 = bf16[128,1024]{1,0:T(8,128)(2,1)} copy(bf16[128,1024]{1,0:T(8,128)(2,1)S(1)} %bitcast.4) | data formatting | bytes 524288
Async XLA Ops:
  0.6 0.7 %copy-start.9 = (f32[256]{0:T(256)S(1)}, f32[256]{0:T(256)}, u32[]{:S(2)}) copy-start(f32[256]{0:T(256)} %param.15) | copy-start | bytes 3076
  0.6 0.7 %copy-start.11 = (s32[128]{0:T(128)S(1)}, s32[128]{0:T(128)}, u32[]{:S(2)}) copy-start(s32[128]{0:T(128)} %param.14) | copy-start | bytes 1540
  0.7 0.7 %copy-start.8 = (s32[2,3]{1,0:T(2,128)S(1)}, s32[2,3]{1,0:T(2,128)}, u32[]{:S(2)}) copy-start(s32[2,3]{1,0:T(2,128)} %tidx_ref.1) | copy-start | bytes 76
  0.7 0.7 %copy-start.10 = (s32[2]{0:T(128)S(1)}, s32[2]{0:T(128)}, u32[]{:S(2)}) copy-start(s32[2]{0:T(128)} %tcnt_ref.1) | copy-start | bytes 28
  1.4 1.0 %copy-start = (bf16[256,1024]{1,0:T(8,128)(2,1)S(1)}, bf16[256,1024]{1,0:T(8,128)(2,1)}, u32[]{:S(2)}) copy-start(bf16[256,1024]{1,0:T(8,128)(2,1)} %og_ref.1) | copy-start | bytes 1572868
  2.4 0.9 %copy-start.1 = (bf16[128,1024]{1,0:T(8,128)(2,1)S(1)}, bf16[128,1024]{1,0:T(8,128)(2,1)}, u32[]{:S(2)}) copy-start(bf16[128,1024]{1,0:T(8,128)(2,1)} %hot_ref.1) | copy-start | bytes 786436
  3.3 0.9 %copy-start.2 = (bf16[128,1024]{1,0:T(8,128)(2,1)S(1)}, bf16[128,1024]{1,0:T(8,128)(2,1)}, u32[]{:S(2)}) copy-start(bf16[128,1024]{1,0:T(8,128)(2,1)} %cold_ref.1) | copy-start | bytes 786436
  4.3 0.9 %copy-start.3 = (bf16[128,1024]{1,0:T(8,128)(2,1)S(1)}, bf16[128,1024]{1,0:T(8,128)(2,1)}, u32[]{:S(2)}) copy-start(bf16[128,1024]{1,0:T(8,128)(2,1)} %stale_ref.1) | copy-start | bytes 786436
  5.2 0.9 %copy-start.4 = (bf16[128,1024]{1,0:T(8,128)(2,1)S(1)}, bf16[128,1024]{1,0:T(8,128)(2,1)}, u32[]{:S(2)}) copy-start(bf16[128,1024]{1,0:T(8,128)(2,1)} %w_ref.1) | copy-start | bytes 786436
  6.2 0.9 %copy-start.5 = (bf16[128,1024]{1,0:T(8,128)(2,1)S(1)}, bf16[128,1024]{1,0:T(8,128)(2,1)}, u32[]{:S(2)}) copy-start(bf16[128,1024]{1,0:T(8,128)(2,1)} %sg_ref.1) | copy-start | bytes 786436
  7.1 0.9 %copy-start.6 = (bf16[2,3,128,128]{3,2,1,0:T(8,128)(2,1)S(1)}, bf16[2,3,128,128]{3,2,1,0:T(8,128)(2,1)}, u32[]{:S(2)}) copy-start(bf16[2,3,128,128]{3,2,1,0:T(8,128)(2,1)} %tile_ref.1) | copy-start | bytes 589828
  8.1 0.7 %copy-start.7 = (s32[8,16]{1,0:T(8,128)S(1)}, s32[8,16]{1,0:T(8,128)}, u32[]{:S(2)}) copy-start(s32[8,16]{1,0:T(8,128)} %send_ref.1) | copy-start | bytes 1540

commit v2 on v1

--- a/solution.py
+++ b/solution.py
@@ -26,18 +26,29 @@
     return nc, sub, blk // sub, depth // nc
 
 
+def flip(value, mask):
+    bit = 1
+    while bit <= mask:
+        if mask & bit:
+            value = value + bit - 2 * bit * (value // bit % 2)
+        bit *= 2
+    return value
+
+
 def mm(a, b):
     return jnp.dot(a, b, preferred_element_type=F32)
 
 
 def kernel(
     n_group, n_dom,
-    tidx_ref, tcnt_ref, hot_ref, cold_ref, sidx_ref, table_ref, stale_ref, tile_ref, w_ref,
-    og_ref, sg_ref, send_ref,
+    tidx_hbm, tcnt_hbm, hot_hbm, cold_hbm, sidx_hbm, table_hbm, stale_hbm, tile_hbm, w_ref,
+    og_hbm, sg_hbm, send_hbm,
     act_ref, fg_ref, wg_ref, nr_ref, ng_ref,
-    src, wbuf, hid, hid_t, pre, ptx, prx, own, stx, rrx, ztx, zrx, ftx, frx, acc, rowsf, outx, bgx,
-    op_hi, op_lo, hgrad,
-    ag_s, ag_r, pa_s, pa_r, nr_s, nr_r, ng_s, ng_r, pt_s, pt_r, st_s, st_r, z_s, z_r, f_s, f_r,
+    tidx_ref, tcnt_ref, cold_ref, sidx_ref, table_ref, tile_ref, og_ref, sg_ref, send_ref,
+    src, wbuf, hid, hid_t, pre, ptx, prx, own, work, stx, rrx, ztx, zrx, ftx, frx, acc, rowsf, outx,
+    bgx, op_hi, op_lo, hgrad,
+    in_s, own_s, ag_s, ag_r, pa_s, pa_r, nr_s, nr_r, ng_s, ng_r, pt_s, pt_r, st_s, st_r, z_s, z_r,
+    f_s, f_r,
 ):
     g, d = lax.axis_index("group"), lax.axis_index("dom")
     n_pair = n_dom // 2
@@ -51,6 +62,14 @@
     peer = send_ref.shape[1]
     sends = n_dom * peer
 
+    bits = n_pair.bit_length() - 1
+
+    loads = [pltpu.make_async_copy(a, b, in_s.at[n]) for n, (a, b) in enumerate((
+        (hot_hbm, src.at[0]), (cold_hbm, cold_ref), (stale_hbm, src.at[2]), (sidx_hbm, sidx_ref),
+        (table_hbm, table_ref), (send_hbm, send_ref), (tile_hbm, tile_ref), (tidx_hbm, tidx_ref),
+        (tcnt_hbm, tcnt_ref), (og_hbm, og_ref), (sg_hbm, sg_ref)))]
+    for load in loads:
+        load.start()
     barrier = pltpu.get_barrier_semaphore()
 
     def hello_dom(r):
@@ -74,25 +93,44 @@
     def cols(ch):
         return pl.ds(pl.multiple_of(ch * cw, cw), cw)
 
-    def ag_copy(ch, r):
-        q = (pair + r) % n_pair
-        return remote(w_ref.at[:, cols(ch)], wbuf.at[ch, d], ag_s.at[ch, r], ag_r.at[ch, r],
-                      {"dom": q * 2 + core})
-
-    def pa_first(ch):
-        return remote(w_ref.at[:, cols(ch)], wbuf.at[ch, d], pa_s.at[ch, 0], pa_r.at[ch, 0],
+    def axis(i, t):
+        return 1 << ((t + i) % bits)
+
+    def near(i, r):
+        return flip(pair, sum(axis(i, t) for t in range(bits) if r >> t & 1))
+
+    def ag_copy(i, r):
+        t = r.bit_length() - 1
+        slot = near(i, r - (1 << t)) * 2 + core
+        source = w_ref.at[:, cols(chunk(i))] if r == 1 << t else wbuf.at[chunk(i), slot]
+        return remote(source, wbuf.at[chunk(i), slot], ag_s.at[i, r], ag_r.at[i, r],
+                      {"dom": near(i, 1 << t) * 2 + core})
+
+    def pa_copy(i, r):
+        slot = near(i, r) * 2 + core
+        source = w_ref.at[:, cols(chunk(i))] if r == 0 else wbuf.at[chunk(i), slot]
+        return remote(source, wbuf.at[chunk(i), slot], pa_s.at[i, r], pa_r.at[i, r],
                       {"dom": partner})
 
-    def pa_copy(ch, r):
-        slot = ((pair - r + n_pair) % n_pair) * 2 + core
-        return remote(wbuf.at[ch, slot], wbuf.at[ch, slot], pa_s.at[ch, r], pa_r.at[ch, r],
-                      {"dom": partner})
+    def keep(i):
+        return pltpu.make_async_copy(w_ref.at[:, cols(chunk(i))], wbuf.at[chunk(i), d], own_s.at[i])
 
     for i in range(nc):
-        each(1, n_pair, lambda r: ag_copy(chunk(i), r).start())
-        pa_first(chunk(i)).start()
+        ag_copy(i, 1).start()
     for i in range(nc):
-        wbuf[i, d] = w_ref[:, i * cw:(i + 1) * cw]
+        for t in range(1, bits):
+            ag_copy(i, 1 << t).start()
+        pa_copy(i, 0).start()
+        keep(i).start()
+    for load in loads[:9]:
+        load.wait()
+
+    def relay(i):
+        for r in range(1, n_pair):
+            ag_copy(i, r).wait_recv()
+            pa_copy(i, r).start()
+            for t in range(r.bit_length(), bits):
+                ag_copy(i, r + (1 << t)).start()
 
     spread = jnp.broadcast_to(sidx_ref[...].astype(F32), (cl, cl)).T
     scale = jnp.zeros((cl, 1), F32)
@@ -100,9 +138,7 @@
         level = (lax.broadcasted_iota(jnp.int32, (cl, cl), 1) + h * cl).astype(F32)
         entry = jnp.broadcast_to(table_ref[:, h * cl:(h + 1) * cl], (cl, cl))
         scale = scale + jnp.sum(jnp.where(spread == level, entry, 0.0), axis=1, keepdims=True)
-    src[0] = hot_ref[...]
     src[1] = (cold_ref[...].astype(F32) * scale).astype(BF16)
-    src[2] = stale_ref[...]
 
     lift = (lax.broadcasted_iota(jnp.int32, (sends, n_dom), 0) // peer
             == lax.broadcasted_iota(jnp.int32, (sends, n_dom), 1)).astype(F32)
@@ -121,6 +157,8 @@
     def nr_copy(r):
         p = (d + r) % n_dom
         return remote(outx.at[p], nr_ref.at[d], nr_s.at[r], nr_r.at[r], {"dom": p})
+
+    relay(0)
 
     for c in range(n_cl):
         total = jnp.zeros((cl, depth), F32)
@@ -145,10 +183,10 @@
     def pt_copy(ch):
         return remote(ptx.at[ch], prx.at[ch], pt_s.at[ch], pt_r.at[ch], {"dom": partner})
 
-    def st_copy(ch, r):
-        q = (pair + r) % n_pair
-        return remote(stx.at[ch, q], rrx.at[ch, r], st_s.at[ch, r], st_r.at[ch, r],
-                      {"dom": q * 2 + core})
+    def st_copy(i, r):
+        low = r & -r
+        return remote(stx.at[i, r], rrx.at[i, r], st_s.at[i, r], st_r.at[i, r],
+                      {"dom": near(i, low) * 2 + core})
 
     def z_copy(r):
         to = (g + r) % n_group
@@ -159,15 +197,14 @@
 
     def stage_a(i):
         ch = chunk(i)
-
-        def relay(r):
-            ag_copy(ch, r).wait_recv()
-            pa_copy(ch, r).start()
-
-        each(1, n_pair, relay)
-        pa_first(ch).wait_recv()
-        each(1, n_pair, lambda r: pa_copy(ch, r).wait_recv())
+        if i + 1 < nc:
+            relay(i + 1)
+        keep(i).wait()
+        for r in range(n_pair):
+            pa_copy(i, r).wait_recv()
         weight = wbuf[ch].reshape(depth, cw)
+        if i == 0:
+            loads[9].wait()
         preact = mm(hid[...], weight)
         s = jax.nn.sigmoid(preact)
         act_ref[:, cols(ch)] = (preact * s).astype(BF16)
@@ -183,18 +220,31 @@
     def stage_b(i):
         ch = chunk(i)
         pt_copy(ch).wait_recv()
-        stx[ch] = (own[ch] + prx[ch].astype(F32)).astype(BF16)
-        each(1, n_pair, lambda r: st_copy(ch, r).start())
-        acc[i] = (own[ch, pair] + prx[ch, pair].astype(F32)).reshape(sub, bs, cw)
+        for r in [*range(1, n_pair, 2), *range(0, n_pair, 2)]:
+            q = near(i, r)
+            both = own[ch, q] + prx[ch, q].astype(F32)
+            if r % 2:
+                stx[i, r] = both.astype(BF16)
+                st_copy(i, r).start()
+            else:
+                work[i, r] = both
+
+    def stage_fold(i, t):
+        step, after = 1 << t, 2 << t
+        for r in [*range(after, n_pair, 2 * after), *range(0, n_pair, 2 * after)]:
+            st_copy(i, r + step).wait_recv()
+            both = work[i, r] + rrx[i, r + step].astype(F32)
+            if r:
+                stx[i, r] = both.astype(BF16)
+                st_copy(i, r).start()
+            else:
+                work[i, r] = both
 
     def stage_c(i):
         ch = chunk(i)
-
-        def add(r):
-            st_copy(ch, r).wait_recv()
-            acc[i] = acc[i] + rrx[ch, r].astype(F32).reshape(sub, bs, cw)
-
-        each(1, n_pair, add)
+        last = n_pair // 2
+        st_copy(i, last).wait_recv()
+        acc[i] = (work[i, 0] + rrx[i, last].astype(F32)).reshape(sub, bs, cw)
         ztx[ch] = acc[i].astype(BF16)
         for h in range(sub):
             if i < nc - 1:
@@ -203,14 +253,24 @@
                 mate = ch * sub + (g + h) % sub
                 z_copy((mate - g + n_group) % n_group).start()
 
+    def step(n):
+        if n == 0:
+            each(1, n_dom, lambda r: nr_copy(r).start())
+        for t in range(-1, bits):
+            i = n - 2 - t
+            if 0 <= i < nc:
+                if t < 0:
+                    stage_b(i)
+                elif t < bits - 1:
+                    stage_fold(i, t)
+                else:
+                    stage_c(i)
+
     for i in range(nc):
         stage_a(i)
-        if i >= 1:
-            stage_b(i - 1)
-        if i == 0:
-            each(1, n_dom, lambda r: nr_copy(r).start())
-        if i >= 2:
-            stage_c(i - 2)
+        if i == 1:
+            loads[10].wait()
+        step(i)
 
     def back(m):
         part = jnp.zeros((rows, cw), F32)
@@ -219,10 +279,11 @@
             part = part + lax.dot_general(pre[c], wpart, NT, preferred_element_type=F32)
         hgrad[:, m * cw:(m + 1) * cw] = part.astype(BF16)
 
+    late = nc
     for m in range(nc):
         back(m)
-        if m == 0:
-            stage_b(nc - 1)
+        if m == nc // 2 - 1:
+            step(late)
 
     def source_grad(j):
         return mm(op_hi[j], hgrad[...]) + mm(op_lo[j], hgrad[...])
@@ -237,9 +298,8 @@
         return remote(bgx.at[p], ng_ref.at[d], ng_s.at[r], ng_r.at[r], {"dom": p})
 
     each(1, n_dom, lambda r: ng_copy(r).start())
-    if nc >= 2:
-        stage_c(nc - 2)
-    stage_c(nc - 1)
+    for n in range(nc + 1, nc + 1 + bits):
+        step(n)
 
     def gather(r):
         z_copy(r).wait_recv()
@@ -275,12 +335,13 @@
         ch = chunk(i)
 
         def drain(r):
-            ag_copy(ch, r).wait_send()
-            pa_copy(ch, r).wait_send()
-            st_copy(ch, r).wait_send()
-
-        each(1, n_pair, drain)
-        pa_first(ch).wait_send()
+            ag_copy(i, r).wait_send()
+            pa_copy(i, r).wait_send()
+            st_copy(i, r).wait_send()
+
+        for r in range(1, n_pair):
+            drain(r)
+        pa_copy(i, 0).wait_send()
         pt_copy(ch).wait_send()
 
     def drain_group(r):
@@ -288,6 +349,15 @@
         f_copy(r).wait_send()
 
     each(1, n_group, drain_group)
+
+
+def write_out(*refs):
+    sems = refs[10]
+    copies = [pltpu.make_async_copy(refs[n], refs[5 + n], sems.at[n]) for n in range(5)]
+    for copy in copies:
+        copy.start()
+    for copy in copies:
+        copy.wait()
 
 
 def local(n_group, n_dom, hot_rows, cold_codes, scale_index, scale_table, stale_rows, tile_index,
@@ -299,7 +369,7 @@
     n_pair = n_dom // 2
     nc, sub, bs, cw = pieces(n_group, blk, depth)
     n_src = rows // cl + stale_rows.shape[0] // cl
-    vmem, smem = pl.BlockSpec(memory_space=pltpu.VMEM), pl.BlockSpec(memory_space=pltpu.SMEM)
+    vmem, hbm = pl.BlockSpec(memory_space=pltpu.VMEM), pl.BlockSpec(memory_space=pltpu.HBM)
     dma = pltpu.SemaphoreType.DMA
     out = pl.pallas_call(
         functools.partial(kernel, n_group, n_dom),
@@ -310,9 +380,18 @@
             jax.ShapeDtypeStruct((n_dom, peer, depth), BF16),
             jax.ShapeDtypeStruct((n_dom, peer, depth), BF16),
         ),
-        in_specs=[smem] * 2 + [vmem] * 10,
+        in_specs=[hbm] * 12,
         out_specs=(vmem,) * 5,
         scratch_shapes=[
+            pltpu.SMEM(tile_index.shape, jnp.int32),
+            pltpu.SMEM(tile_count.shape, jnp.int32),
+            pltpu.VMEM(cold_codes.shape, BF16),
+            pltpu.VMEM((1, scale_index.shape[0]), jnp.int32),
+            pltpu.VMEM((1, scale_table.shape[0]), F32),
+            pltpu.VMEM(tile_values.shape, BF16),
+            pltpu.VMEM(out_grad.shape, BF16),
+            pltpu.VMEM(stale_grads.shape, BF16),
+            pltpu.VMEM(send_rows.shape, jnp.int32),
             pltpu.VMEM((n_src, cl, depth), BF16),
             pltpu.VMEM((nc, n_dom, blk, cw), BF16),
             pltpu.VMEM((rows, depth), BF16),
@@ -320,6 +399,7 @@
             pltpu.VMEM((nc, rows, cw), BF16),
             pltpu.VMEM((nc, n_pair, blk, cw), BF16),
             pltpu.VMEM((nc, n_pair, blk, cw), BF16),
+            pltpu.VMEM((nc, n_pair, blk, cw), F32),
             pltpu.VMEM((nc, n_pair, blk, cw), F32),
             pltpu.VMEM((nc, n_pair, blk, cw), BF16),
             pltpu.VMEM((nc, n_pair, blk, cw), BF16),
@@ -334,6 +414,7 @@
             pltpu.VMEM((n_src, cl, rows), BF16),
             pltpu.VMEM((n_src, cl, rows), BF16),
             pltpu.VMEM((rows, depth), BF16),
+            dma((11,)), dma((nc,)),
             dma((nc, n_pair)), dma((nc, n_pair)), dma((nc, n_pair)), dma((nc, n_pair)),
             dma((n_dom,)), dma((n_dom,)), dma((n_dom,)), dma((n_dom,)),
             dma((nc,)), dma((nc,)), dma((nc, n_pair)), dma((nc, n_pair)),
@@ -341,9 +422,18 @@
         ],
         compiler_params=pltpu.CompilerParams(
             collective_id=0, has_side_effects=True, vmem_limit_bytes=48 * 1024 * 1024),
-    )(tile_index, tile_count, hot_rows, cold_codes, scale_index.reshape(1, -1),
-      scale_table.reshape(1, -1), stale_rows, tile_values, weight, out_grad, stale_grads, send_rows)
-    act, fg, wg, nr, ng = out
+    )(*[pltpu.with_memory_space_constraint(a, pltpu.HBM) for a in (
+        tile_index, tile_count, hot_rows, cold_codes, scale_index.reshape(1, -1),
+        scale_table.reshape(1, -1), stale_rows, tile_values, weight, out_grad, stale_grads,
+        send_rows)])
+    act, fg, wg, nr, ng = pl.pallas_call(
+        write_out,
+        out_shape=tuple(jax.ShapeDtypeStruct(o.shape, o.dtype) for o in out),
+        in_specs=[vmem] * 5,
+        out_specs=(hbm,) * 5,
+        scratch_shapes=[dma((5,))],
+        compiler_params=pltpu.CompilerParams(vmem_limit_bytes=8 * 1024 * 1024),
+    )(*out)
     return act, fg, wg, nr.reshape(-1, depth), ng.reshape(-1, depth)
 
 

time: 57.4 us -> 56.4 us (0.983)
  local copies, waits for them, and re-layouts: 11.9 us -> 0 us
  Pallas kernels: 44.5 us -> 55.6 us
    unnamed x29 -> x0, local copies, waits for them, and re-layouts: 11.9 us -> none
    pallas_call x1, Pallas kernels: 44.5 us -> 54.3 us  [local(): pl.pallas_call(functools.partial(kernel, n_group, n_dom), out_shape=(jax....]
    pallas_call x0 -> x1, Pallas kernels: none -> 1.35 us  [local(): pl.pallas_call(write_out, out_shape=tuple((jax.ShapeDtypeStruct(o.shape,...]
where the time goes in v2:
time: 56.4 us; the launch traced here: 56.3 us
  Pallas kernels  55.6 us (99%)
  between operations  0.64 us (1%)
    pallas_call x1, Pallas kernels, local(): pl.pallas_call(functools.partial(kernel, n_group, n_dom), out_shape=(jax....  54.3 us
    pallas_call x1, Pallas kernels, local(): pl.pallas_call(write_out, out_shape=tuple((jax.ShapeDtypeStruct(o.shape,...  1.35 us

profile of v2, /device:TPU:0, one launch (start us, length us, event | category | flops | bytes accessed | tf_op | source)
XLA Modules:
  0.0 56.3 jit_solution(5739670796410313801)
XLA Ops:
  0.6 54.3 %shard_map.155 = (bf16[256,1024]{1,0:T(8,128)(2,1)S(1)}, bf16[256,1024]{1,0:T(8,128)(2,1)S(1)}, f32[128,1024]{1,0:T(8,128)S(1)}, bf16[8,16,1024]{2,1,0:T(8,128)(2,1)S(1)}, bf16[8,16,1024]{2,1,0:T(8,128)(2,1)S(1)}) custom-call(s32[2,3]{1,0:T(2,128)} %tidx_hbm.1, s32[2]{0:T(128)} %tcnt_hbm.1, bf16[128,1024]{1,0:T(8,128)(2,1)} %hot_hbm.1, ...), custom_call_target="tpu_custom_call" | custom-call | tf_op jit(solution)/shard_map/pallas_call | solution.py:374
  54.9 1.4 %shard_map.156 = (bf16[256,1024]{1,0:T(8,128)(2,1)}, bf16[256,1024]{1,0:T(8,128)(2,1)}, f32[128,1024]{1,0:T(8,128)}, bf16[8,16,1024]{2,1,0:T(8,128)(2,1)}, bf16[8,16,1024]{2,1,0:T(8,128)(2,1)}) custom-call(bf16[256,1024]{1,0:T(8,128)(2,1)S(1)} %get-tuple-element.15.refs_0_, bf16[256,1024]{1,0:T(8,128)(2,1)S(1)} %get-tuple-element.16.refs_1_, ...), custom_call_target="tpu_custom_call" | custom-call | tf_op jit(solution)/shard_map/pallas_call | solution.py:429

commit v3 on v2

--- a/solution.py
+++ b/solution.py
@@ -47,7 +47,7 @@
     tidx_ref, tcnt_ref, cold_ref, sidx_ref, table_ref, tile_ref, og_ref, sg_ref, send_ref,
     src, wbuf, hid, hid_t, pre, ptx, prx, own, work, stx, rrx, ztx, zrx, ftx, frx, acc, rowsf, outx,
     bgx, op_hi, op_lo, hgrad,
-    in_s, own_s, ag_s, ag_r, pa_s, pa_r, nr_s, nr_r, ng_s, ng_r, pt_s, pt_r, st_s, st_r, z_s, z_r,
+    in_s, own_s, ag_s, ag_r, zw_s, zw_r, pa_s, pa_r, nr_s, nr_r, ng_s, ng_r, pt_s, pt_r, st_s, st_r, z_s, z_r,
     f_s, f_r,
 ):
     g, d = lax.axis_index("group"), lax.axis_index("dom")
@@ -88,23 +88,30 @@
             device_id=where, device_id_type=MESH)
 
     def chunk(i):
-        return (g // sub + 1 + i) % nc
+        return flip(g // sub, (i + 1) % nc)
 
     def cols(ch):
         return pl.ds(pl.multiple_of(ch * cw, cw), cw)
 
     def axis(i, t):
-        return 1 << ((t + i) % bits)
+        return 1 << t
 
     def near(i, r):
         return flip(pair, sum(axis(i, t) for t in range(bits) if r >> t & 1))
 
     def ag_copy(i, r):
-        t = r.bit_length() - 1
-        slot = near(i, r - (1 << t)) * 2 + core
-        source = w_ref.at[:, cols(chunk(i))] if r == 1 << t else wbuf.at[chunk(i), slot]
-        return remote(source, wbuf.at[chunk(i), slot], ag_s.at[i, r], ag_r.at[i, r],
-                      {"dom": near(i, 1 << t) * 2 + core})
+        return remote(w_ref.at[:, cols(chunk(i))], wbuf.at[chunk(i), d], ag_s.at[i, r],
+                      ag_r.at[i, r], {"dom": near(i, r) * 2 + core})
+
+    def zw_copy(r):
+        slot = near(0, r) * 2 + core
+        return remote(wbuf.at[chunk(0), slot], wbuf.at[chunk(0), slot], zw_s.at[r], zw_r.at[r],
+                      {"group": flip(g, sub)})
+
+    def zw_in(r):
+        slot = near(0, r) * 2 + core
+        return remote(wbuf.at[chunk(nc - 1), slot], wbuf.at[chunk(nc - 1), slot], zw_s.at[r],
+                      zw_r.at[r], {"group": flip(g, sub)})
 
     def pa_copy(i, r):
         slot = near(i, r) * 2 + core
@@ -115,11 +122,10 @@
     def keep(i):
         return pltpu.make_async_copy(w_ref.at[:, cols(chunk(i))], wbuf.at[chunk(i), d], own_s.at[i])
 
+    for i in range(nc - 1):
+        for r in range(1, n_pair):
+            ag_copy(i, r).start()
     for i in range(nc):
-        ag_copy(i, 1).start()
-    for i in range(nc):
-        for t in range(1, bits):
-            ag_copy(i, 1 << t).start()
         pa_copy(i, 0).start()
         keep(i).start()
     for load in loads[:9]:
@@ -127,10 +133,13 @@
 
     def relay(i):
         for r in range(1, n_pair):
-            ag_copy(i, r).wait_recv()
+            if i < nc - 1:
+                ag_copy(i, r).wait_recv()
+            else:
+                zw_in(r).wait_recv()
+            if i == 0:
+                zw_copy(r).start()
             pa_copy(i, r).start()
-            for t in range(r.bit_length(), bits):
-                ag_copy(i, r + (1 << t)).start()
 
     spread = jnp.broadcast_to(sidx_ref[...].astype(F32), (cl, cl)).T
     scale = jnp.zeros((cl, 1), F32)
@@ -184,7 +193,7 @@
         return remote(ptx.at[ch], prx.at[ch], pt_s.at[ch], pt_r.at[ch], {"dom": partner})
 
     def st_copy(i, r):
-        low = r & -r
+        low = r
         return remote(stx.at[i, r], rrx.at[i, r], st_s.at[i, r], st_r.at[i, r],
                       {"dom": near(i, low) * 2 + core})
 
@@ -197,8 +206,8 @@
 
     def stage_a(i):
         ch = chunk(i)
-        if i + 1 < nc:
-            relay(i + 1)
+        if i:
+            relay(i)
         keep(i).wait()
         for r in range(n_pair):
             pa_copy(i, r).wait_recv()
@@ -220,31 +229,22 @@
     def stage_b(i):
         ch = chunk(i)
         pt_copy(ch).wait_recv()
-        for r in [*range(1, n_pair, 2), *range(0, n_pair, 2)]:
+        for r in [*range(1, n_pair), 0]:
             q = near(i, r)
             both = own[ch, q] + prx[ch, q].astype(F32)
-            if r % 2:
-                stx[i, r] = both.astype(BF16)
-                st_copy(i, r).start()
-            else:
-                work[i, r] = both
-
-    def stage_fold(i, t):
-        step, after = 1 << t, 2 << t
-        for r in [*range(after, n_pair, 2 * after), *range(0, n_pair, 2 * after)]:
-            st_copy(i, r + step).wait_recv()
-            both = work[i, r] + rrx[i, r + step].astype(F32)
             if r:
                 stx[i, r] = both.astype(BF16)
                 st_copy(i, r).start()
             else:
-                work[i, r] = both
+                work[i] = both
 
     def stage_c(i):
         ch = chunk(i)
-        last = n_pair // 2
-        st_copy(i, last).wait_recv()
-        acc[i] = (work[i, 0] + rrx[i, last].astype(F32)).reshape(sub, bs, cw)
+        total = work[i]
+        for r in range(1, n_pair):
+            st_copy(i, r).wait_recv()
+            total = total + rrx[i, r].astype(F32)
+        acc[i] = total.reshape(sub, bs, cw)
         ztx[ch] = acc[i].astype(BF16)
         for h in range(sub):
             if i < nc - 1:
@@ -254,17 +254,10 @@
                 z_copy((mate - g + n_group) % n_group).start()
 
     def step(n):
-        if n == 0:
-            each(1, n_dom, lambda r: nr_copy(r).start())
-        for t in range(-1, bits):
-            i = n - 2 - t
-            if 0 <= i < nc:
-                if t < 0:
-                    stage_b(i)
-                elif t < bits - 1:
-                    stage_fold(i, t)
-                else:
-                    stage_c(i)
+        if 0 <= n - 1 < nc:
+            stage_b(n - 1)
+        if 0 <= n - 2 < nc:
+            stage_c(n - 2)
 
     for i in range(nc):
         stage_a(i)
@@ -297,9 +290,14 @@
         p = (d + r) % n_dom
         return remote(bgx.at[p], ng_ref.at[d], ng_s.at[r], ng_r.at[r], {"dom": p})
 
-    each(1, n_dom, lambda r: ng_copy(r).start())
-    for n in range(nc + 1, nc + 1 + bits):
+    for n in range(nc + 1, nc + 2):
         step(n)
+
+    def swap(r):
+        nr_copy(r).start()
+        ng_copy(r).start()
+
+    each(1, n_dom, swap)
 
     def gather(r):
         z_copy(r).wait_recv()
@@ -335,7 +333,10 @@
         ch = chunk(i)
 
         def drain(r):
-            ag_copy(i, r).wait_send()
+            if i < nc - 1:
+                ag_copy(i, r).wait_send()
+            else:
+                zw_copy(r).wait_send()
             pa_copy(i, r).wait_send()
             st_copy(i, r).wait_send()
 
@@ -400,7 +401,7 @@
             pltpu.VMEM((nc, n_pair, blk, cw), BF16),
             pltpu.VMEM((nc, n_pair, blk, cw), BF16),
             pltpu.VMEM((nc, n_pair, blk, cw), F32),
-            pltpu.VMEM((nc, n_pair, blk, cw), F32),
+            pltpu.VMEM((nc, blk, cw), F32),
             pltpu.VMEM((nc, n_pair, blk, cw), BF16),
             pltpu.VMEM((nc, n_pair, blk, cw), BF16),
             pltpu.VMEM((nc, sub, bs, cw), BF16),
@@ -415,7 +416,7 @@
             pltpu.VMEM((n_src, cl, rows), BF16),
             pltpu.VMEM((rows, depth), BF16),
             dma((11,)), dma((nc,)),
-            dma((nc, n_pair)), dma((nc, n_pair)), dma((nc, n_pair)), dma((nc, n_pair)),
+            dma((nc, n_pair)), dma((nc, n_pair)), dma((n_pair,)), dma((n_pair,)), dma((nc, n_pair)), dma((nc, n_pair)),
             dma((n_dom,)), dma((n_dom,)), dma((n_dom,)), dma((n_dom,)),
             dma((nc,)), dma((nc,)), dma((nc, n_pair)), dma((nc, n_pair)),
             dma((n_group,)), dma((n_group,)), dma((n_group,)), dma((n_group,)),

time: 56.4 us -> 42.8 us (0.76)
  Pallas kernels: 55.6 us -> 42 us
    pallas_call x1, Pallas kernels: 54.3 us -> 40.7 us  [local(): pl.pallas_call(functools.partial(kernel, n_group, n_dom), out_shape=(jax....]
where the time goes in v3:
time: 42.8 us; the launch traced here: 42.7 us
  Pallas kernels  42 us (98%)
  between operations  0.64 us (1%)
    pallas_call x1, Pallas kernels, local(): pl.pallas_call(functools.partial(kernel, n_group, n_dom), out_shape=(jax....  40.7 us
    pallas_call x1, Pallas kernels, local(): pl.pallas_call(write_out, out_shape=tuple((jax.ShapeDtypeStruct(o.shape,...  1.35 us

profile of v3, /device:TPU:0, one launch (start us, length us, event | category | flops | bytes accessed | tf_op | source)
XLA Modules:
  0.0 42.7 jit_solution(5180599622459645291)
XLA Ops:
  0.6 40.7 %shard_map.155 = (bf16[256,1024]{1,0:T(8,128)(2,1)S(1)}, bf16[256,1024]{1,0:T(8,128)(2,1)S(1)}, f32[128,1024]{1,0:T(8,128)S(1)}, bf16[8,16,1024]{2,1,0:T(8,128)(2,1)S(1)}, bf16[8,16,1024]{2,1,0:T(8,128)(2,1)S(1)}) custom-call(s32[2,3]{1,0:T(2,128)} %tidx_hbm.1, s32[2]{0:T(128)} %tcnt_hbm.1, bf16[128,1024]{1,0:T(8,128)(2,1)} %hot_hbm.1, ...), custom_call_target="tpu_custom_call" | custom-call | tf_op jit(solution)/shard_map/pallas_call | solution.py:375
  41.3 1.4 %shard_map.156 = (bf16[256,1024]{1,0:T(8,128)(2,1)}, bf16[256,1024]{1,0:T(8,128)(2,1)}, f32[128,1024]{1,0:T(8,128)}, bf16[8,16,1024]{2,1,0:T(8,128)(2,1)}, bf16[8,16,1024]{2,1,0:T(8,128)(2,1)}) custom-call(bf16[256,1024]{1,0:T(8,128)(2,1)S(1)} %get-tuple-element.15.refs_0_, bf16[256,1024]{1,0:T(8,128)(2,1)S(1)} %get-tuple-element.16.refs_1_, ...), custom_call_target="tpu_custom_call" | custom-call | tf_op jit(solution)/shard_map/pallas_call | solution.py:430
